TPU v7x, 256 devices: a whole 4x4x8 slice. The times are simulated.
256 devices in a mesh: depth: 64 (over x, y, z_hi), comp: 4 (over z_lo, core).
Axes of the slice: x: 4, y: 4, z: 8 (z_hi: 4, z_lo: 2; z = z_hi * 2 + z_lo), core: 2. Of those that a mesh axis runs over, the one named last changes fastest.
Arguments:
- density: float32 [64, 512, 256], P('depth', 'comp'), may hold values from -4 to 4
- observed: float32 [4, 512, 256], P('comp', 'depth'), may hold values from -6 to 6
- data_weight: float32 [4, 512, 256], P('comp', 'depth'), may hold values from 0.3 to 7.5
- layer_top: float32 [64], P('depth'), may hold values from 0.5 to 8
Outputs:
- density_new: float32 [64, 512, 256], P('depth', 'comp')
- weighted_error: float32 [4, 512, 256], P('comp', 'depth')
All inputs are finite; a program needn't handle non-finite values.
Results may differ from a plain program's by a relative error of at most 0.0001.
Values sent between devices are 32-bit elements; how exact they have to be, the bound alone decides.
No kernel may reach another device: no remote copies, remote signals or barrier semaphores. Data moves between devices by JAX's collectives and lax.ppermute only.
A program may use at most 64 MiB of HBM per device.

v0:
```python
import math
import jax
import jax.numpy as jnp
from jax import lax
from jax.sharding import PartitionSpec as P

ITERS = 2
TWO_PI = 2.0 * math.pi


def matmul(left, right):
    return jnp.dot(left, right, precision=lax.Precision.HIGHEST, preferred_element_type=jnp.float32)


def tables(count):
    index = lax.iota(jnp.int32, count)
    product = index[:, None] * index[None, :] % count
    angle = product.astype(jnp.float32) * (TWO_PI / count)
    return (jnp.cos(angle), jnp.sin(angle))


def wavenumbers(count):
    index = lax.iota(jnp.int32, count)
    signed = jnp.where(index < (count - 1) // 2 + 1, index, index - count)
    return signed.astype(jnp.float32) * (TWO_PI / count)


def kernel_parts(top, comp_index, rows_all, cols_all):
    kx = wavenumbers(rows_all)[:, None]
    ky = wavenumbers(cols_all)[None, :]
    kabs = jnp.sqrt(kx * kx + ky * ky)
    floor_k = jnp.maximum(kabs, TWO_PI / max(rows_all, cols_all))
    decay = 4.0 * jnp.exp(-kabs * top) * (1.0 - jnp.exp(-kabs))
    zeros = jnp.zeros_like(kabs)
    real_part = jnp.where(
        comp_index == 0,
        decay,
        jnp.where(comp_index == 3, decay * (-(kx * kx) / (floor_k * floor_k)), zeros),
    )
    imag_part = jnp.where(
        comp_index == 1,
        decay * (kx / floor_k),
        jnp.where(comp_index == 2, decay * (ky / floor_k), zeros),
    )
    return (real_part, imag_part)


def along_rows(field, cos_y, sin_y):
    return (matmul(field, cos_y), -matmul(field, sin_y))


def add_columns(part_re, part_im, cos_cols, sin_cols):
    new_re = matmul(cos_cols, part_re) + matmul(sin_cols, part_im)
    new_im = matmul(cos_cols, part_im) - matmul(sin_cols, part_re)
    return (new_re, new_im)


def inverse_rows(spec_re, spec_im, cos_rows, sin_rows, cos_y, sin_y, scale):
    mixed_re = matmul(cos_rows, spec_re) - matmul(sin_rows, spec_im)
    mixed_im = matmul(cos_rows, spec_im) + matmul(sin_rows, spec_re)
    return (matmul(mixed_re, cos_y) - matmul(mixed_im, sin_y)) * scale


def body(density, observed, data_weight, layer_top):
    own_rows = density.shape[1]
    comps = lax.axis_size("comp")
    rows_all = own_rows * comps
    cols_all = density.shape[2]
    comp_index = lax.axis_index("comp")
    cos_x, sin_x = tables(rows_all)
    cos_y, sin_y = tables(cols_all)
    scale = 1.0 / (rows_all * cols_all)
    kernels = [kernel_parts(layer_top[0], comp_index, rows_all, cols_all)]
    weight = data_weight[0]
    measured = observed[0]

    def spectrum(field):
        part_re, part_im = along_rows(field, cos_y, sin_y)
        return add_columns(part_re, part_im, cos_x, sin_x)

    def forward_once(fields):
        spec_re, spec_im = spectrum(fields[0])
        kre, kim = kernels[0]
        total_re = kre * spec_re - kim * spec_im
        total_im = kre * spec_im + kim * spec_re
        return lax.psum_scatter(
            inverse_rows(total_re, total_im, cos_x, sin_x, cos_y, sin_y, scale),
            "depth",
            scatter_dimension=0,
            tiled=True,
        )

    def forward(fields):
        return forward_once(fields)

    dens_full = lax.all_gather(density, "comp", axis=1, tiled=True)
    dens_strip = density
    predicted = forward([dens_full[0]])
    weighted_error = weight * (predicted - measured)
    for step in range(ITERS):
        weighted_res = weight * weighted_error
        add_part_re, add_part_im = along_rows(
            lax.all_gather(weighted_res, "depth", axis=0, tiled=True), cos_y, sin_y
        )
        res_re, res_im = add_columns(add_part_re, add_part_im, cos_x, sin_x)
        kre, kim = kernels[0]
        grad_re = kre * res_re + kim * res_im
        grad_im = kre * res_im - kim * res_re
        terms = [inverse_rows(grad_re, grad_im, cos_x, sin_x, cos_y, sin_y, scale)]
        data_grad = jnp.stack(terms)
        quad_strip = 1.0 / (dens_strip * dens_strip + 0.25)
        grad_strip = lax.psum_scatter(data_grad, "comp", scatter_dimension=1, tiled=True) + 0.5 * (
            quad_strip * dens_strip
        )
        grad_full = lax.all_gather(grad_strip, "comp", axis=1, tiled=True)
        grad_sq = jnp.sum(grad_strip * grad_strip)
        quad_sq = jnp.sum(quad_strip * grad_strip * grad_strip)
        grad_sq, quad_sq = lax.psum((grad_sq, quad_sq), ("depth", "comp"))
        image = forward([grad_full[0]])
        weighted_image = weight * image
        curv = jnp.sum(weighted_image * weighted_image)
        curv = lax.psum(curv, ("depth", "comp"))
        alpha = grad_sq / (curv + 0.5 * quad_sq)
        dens_strip = dens_strip - alpha * grad_strip
        predicted = predicted - alpha * image
        weighted_error = weight * (predicted - measured)
    return (dens_strip, weighted_error[None])


def solution(mesh):
    return jax.shard_map(
        body,
        mesh=mesh,
        in_specs=(
            P("depth", "comp", None),
            P("comp", "depth", None),
            P("comp", "depth", None),
            P("depth"),
        ),
        out_specs=(P("depth", "comp", None), P("comp", "depth", None)),
        check_vma=False,
    )
```

profile of v0, /device:TPU:1, one launch (start us, length us, event | category | flops | bytes accessed | tf_op | source)
XLA Modules:
  0.0 2017.7 jit_solution(2522826895115508715)
XLA Ops:
  7.3 9.8 all_gather.15
  52.4 5.7 convolution_subtract_fusion.8
  59.6 5.9 convolution_add_fusion.8
  68.0 334.6 %reduce-scatter.6.cloned.1.call-done = f32[8,256]{1,0:T(8,128)} async-done(((f32[512,256]{1,0:T(8,128)}), f32[8,256]{1,0:T(8,128)}) %reduce-scatter.6.cloned.1.call-update) | async-done | bytes 8208 | tf_op jit(solution)/shard_map/reduce_scatter | solution.py:86
  403.3 161.1 %all_gather.16 = f32[512,256]{1,0:T(8,128)S(1)} all-gather(f32[8,256]{1,0:T(8,128)S(1)} %multiply_multiply_fusion.3), channel_id=1, replica_groups=mesh['depth'=64,'comp'=4] {'depth'}, dimensions={0}, use_global_device_ids=true | all-gather | bytes 532480 | tf_op jit(solution)/shard_map/all_gather | solution.py:103
  584.5 5.8 convolution_subtract_fusion.7
  601.2 5.7 convolution_subtract_fusion.6
  608.5 5.9 convolution_add_fusion.6
  616.9 93.4 %reduce-scatter.8.cloned.1.call-done = f32[1,128,256]{2,1,0:T(8,128)} async-done(((f32[1,512,256]{2,1,0:T(8,128)}), f32[1,128,256]{2,1,0:T(8,128)}) %reduce-scatter.8.cloned.1.call-update) | async-done | bytes 131088 | tf_op jit(solution)/shard_map/reduce_scatter | solution.py:112
  711.9 7.3 all_gather.17
  739.1 5.8 convolution_subtract_fusion.5
  763.2 5.9 convolution_add_fusion.4
  771.5 333.5 %reduce-scatter.10.cloned.1.call-done = f32[8,256]{1,0:T(8,128)} async-done(((f32[512,256]{1,0:T(8,128)}), f32[8,256]{1,0:T(8,128)}) %reduce-scatter.10.cloned.1.call-update) | async-done | bytes 8208 | tf_op jit(solution)/shard_map/reduce_scatter | solution.py:86
  1106.4 123.9 %all-reduce.1 = (f32[]{:T(128)}, f32[]{:T(128)}, f32[]{:T(128)}) all-reduce(f32[]{:T(128)} %get-tuple-element.5, f32[]{:T(128)} %fusion.127, f32[]{:T(128)} %get-tuple-element.4), channel_id=1, replica_groups=mesh['depth'=64,'comp'=4] {'depth','comp'}, use_global_device_ids=true, to_apply=%region_3.4 | all-reduce | flops 3 | bytes 24 | tf_op jit(solution)/shard_map/psum | solution.py:118
  1232.1 161.9 %all_gather.18 = f32[512,256]{1,0:T(8,128)S(1)} all-gather(f32[8,256]{1,0:T(8,128)S(1)} %multiply_multiply_fusion.2), channel_id=1, replica_groups=mesh['depth'=64,'comp'=4] {'depth'}, dimensions={0}, use_global_device_ids=true | all-gather | bytes 532480 | tf_op jit(solution)/shard_map/all_gather | solution.py:103
  1414.0 5.8 convolution_subtract_fusion.3
  1430.8 5.7 convolution_subtract_fusion.2
  1438.1 5.9 convolution_add_fusion.2
  1446.4 41.4 %reduce-scatter.12.cloned.1.call-done = f32[1,128,256]{2,1,0:T(8,128)} async-done(((f32[1,512,256]{2,1,0:T(8,128)}), f32[1,128,256]{2,1,0:T(8,128)}) %reduce-scatter.12.cloned.1.call-update) | async-done | bytes 131088 | tf_op jit(solution)/shard_map/reduce_scatter | solution.py:112
  1489.4 7.3 all_gather.19
  1516.6 5.8 convolution_subtract_fusion.1
  1540.7 5.8 convolution_add_fusion
  1548.8 333.5 %reduce-scatter.14.cloned.1.call-done = f32[8,256]{1,0:T(8,128)} async-done(((f32[512,256]{1,0:T(8,128)}), f32[8,256]{1,0:T(8,128)}) %reduce-scatter.14.cloned.1.call-update) | async-done | bytes 8208 | tf_op jit(solution)/shard_map/reduce_scatter | solution.py:86
  1883.6 123.9 %all-reduce = (f32[]{:T(128)}, f32[]{:T(128)}, f32[]{:T(128)}) all-reduce(f32[]{:T(128)} %get-tuple-element.3, f32[]{:T(128)} %fusion.125, f32[]{:T(128)} %get-tuple-element.2), channel_id=1, replica_groups=mesh['depth'=64,'comp'=4] {'depth','comp'}, use_global_device_ids=true, to_apply=%region_11.12 | all-reduce | flops 3 | bytes 24 | tf_op jit(solution)/shard_map/psum | solution.py:118
  (81 shorter events, 197.4 us)
Async XLA Ops:
  7.2 395.5 %reduce-scatter.6.cloned.1.call-start = ((), (), s32[]{:S(2)}) async-start(), calls=%async_computation.5 | async-start | bytes 532480 | tf_op jit(solution)/shard_map/reduce_scatter | solution.py:86
  67.9 334.7 %copy-start.1 = (f32[1,8,256]{2,1,0:T(8,128)S(1)}, f32[1,8,256]{2,1,0:T(8,128)}, u32[]{:S(2)}) copy-start(f32[1,8,256]{2,1,0:T(8,128)} %param.6) | copy-start | bytes 24580
  67.9 334.7 %copy-start.3 = (f32[1,8,256]{2,1,0:T(8,128)S(1)}, f32[1,8,256]{2,1,0:T(8,128)}, u32[]{:S(2)}) copy-start(f32[1,8,256]{2,1,0:T(8,128)} %param.5) | copy-start | bytes 24580
  68.0 642.3 %reduce-scatter.8.cloned.1.call-start = ((), (), s32[]{:S(2)}) async-start(), calls=%async_computation.6 | async-start | bytes 655360 | tf_op jit(solution)/shard_map/reduce_scatter | solution.py:112
  616.8 93.4 %copy-start = (f32[1,128,256]{2,1,0:T(8,128)S(1)}, f32[1,128,256]{2,1,0:T(8,128)}, u32[]{:S(2)}) copy-start(f32[1,128,256]{2,1,0:T(8,128)} %param.4) | copy-start | bytes 393220
  616.8 488.1 %reduce-scatter.10.cloned.1.call-start = ((), (), s32[]{:S(2)}) async-start(), calls=%async_computation.7 | async-start | bytes 532480 | tf_op jit(solution)/shard_map/reduce_scatter | solution.py:86
  771.5 716.3 %reduce-scatter.12.cloned.1.call-start = ((), (), s32[]{:S(2)}) async-start(), calls=%async_computation.8 | async-start | bytes 655360 | tf_op jit(solution)/shard_map/reduce_scatter | solution.py:112
  1106.3 125.8 %copy-start.4 = (f32[8,256]{1,0:T(8,128)S(1)}, f32[8,256]{1,0:T(8,128)}, u32[]{:S(2)}) copy-start(f32[8,256]{1,0:T(8,128)} %reduce-scatter.6.cloned.1.call-done) | copy-start | bytes 24580
  1106.4 125.8 %copy-start.2 = (f32[8,256]{1,0:T(8,128)S(1)}, f32[8,256]{1,0:T(8,128)}, u32[]{:S(2)}) copy-start(f32[8,256]{1,0:T(8,128)} %reduce-scatter.10.cloned.1.call-done) | copy-start | bytes 24580
  1446.4 436.0 %reduce-scatter.14.cloned.1.call-start = ((), (), s32[]{:S(2)}) async-start(), calls=%async_computation.9 | async-start | bytes 532480 | tf_op jit(solution)/shard_map/reduce_scatter | solution.py:86
  2009.4 0.7 copy-start.5
Sparse Core Ops, SparseCore 0:
  68.1 334.4 reduce-scatter.5
  616.9 93.2 reduce-scatter.7
  771.6 333.3 reduce-scatter.9
  1446.5 41.2 reduce-scatter.11
  1548.9 333.3 reduce-scatter.13
where the time goes:
time: 2030 us; the launch traced here: 2020 us
  waiting for transfers between devices  1140 us (56%)
  blocking collectives  595 us (29%)
  matrix products  259 us (13%)
    reduce_scatter x3, waiting for transfers between devices, forward_once(): lax.psum_scatter(inverse_rows(total_re, total_im, cos_x, sin_x, cos_y, si...  1000 us
    all_gather x2, blocking collectives, body(): lax.all_gather(weighted_res, 'depth', axis=0, tiled=True)  323 us
    dot_general x60, matrix products, matmul(): jnp.dot(left, right, precision=lax.Precision.HIGHEST, preferred_element_t...  259 us
    psum x2, blocking collectives, body(): grad_sq, quad_sq = lax.psum((grad_sq, quad_sq), ('depth', 'comp'))  248 us
    reduce_scatter x2, waiting for transfers between devices, body(): lax.psum_scatter(data_grad, 'comp', scatter_dimension=1, tiled=True)  135 us
  transfers between devices with their start and end apart: 5, of which 5 were waited for; matrix products, arithmetic and copies ran while one was open for 0% of the time, Pallas kernels for 0%

commit v1 on v0

--- a/solution.py
+++ b/solution.py
@@ -100,7 +100,12 @@
     for step in range(ITERS):
         weighted_res = weight * weighted_error
         add_part_re, add_part_im = along_rows(
-            lax.all_gather(weighted_res, "depth", axis=0, tiled=True), cos_y, sin_y
+            jnp.concatenate(
+                lax.all_to_all(jnp.stack([weighted_res] * lax.axis_size("depth")), "depth", 0, 0),
+                axis=0,
+            ),
+            cos_y,
+            sin_y,
         )
         res_re, res_im = add_columns(add_part_re, add_part_im, cos_x, sin_x)
         kre, kim = kernels[0]

time: 2030 us -> 1700 us (0.84)
  blocking collectives: 595 us -> 316 us
  waiting for transfers between devices: 1140 us -> 1090 us
    all_gather x2 -> x0, blocking collectives: 323 us -> none  [body(): lax.all_gather(weighted_res, 'depth', axis=0, tiled=True)]
    reduce_scatter x2, waiting for transfers between devices: 135 us -> 90.1 us  [body(): lax.psum_scatter(data_grad, 'comp', scatter_dimension=1, tiled=True)]
    all_to_all x0 -> x2, blocking collectives: none -> 42.9 us  [body(): lax.all_to_all(jnp.stack([weighted_res] * lax.axis_size('depth')), 'depth...]
where the time goes in v1:
time: 1700 us
  waiting for transfers between devices  1090 us (64%)
  blocking collectives  316 us (19%)
  matrix products  259 us (15%)
  between operations  19.1 us (1%)
    reduce_scatter x3, waiting for transfers between devices, forward_once(): lax.psum_scatter(inverse_rows(total_re, total_im, cos_x, sin_x, cos_y, si...  1000 us
    dot_general x60, matrix products, matmul(): jnp.dot(left, right, precision=lax.Precision.HIGHEST, preferred_element_t...  259 us
    psum x2, blocking collectives, body(): grad_sq, quad_sq = lax.psum((grad_sq, quad_sq), ('depth', 'comp'))  248 us
    reduce_scatter x2, waiting for transfers between devices, body(): lax.psum_scatter(data_grad, 'comp', scatter_dimension=1, tiled=True)  90.1 us
    all_to_all x2, blocking collectives, body(): lax.all_to_all(jnp.stack([weighted_res] * lax.axis_size('depth')), 'depth...  42.9 us
  transfers between devices with their start and end apart: 5, of which 5 were waited for; matrix products, arithmetic and copies ran while one was open for 0% of the time, Pallas kernels for 0%

profile of v1, /device:TPU:1, one launch (start us, length us, event | category | flops | bytes accessed | tf_op | source)
XLA Modules:
  0.0 1695.1 jit_solution(3875936726062198256)
XLA Ops:
  7.3 9.8 all_gather.9
  52.4 5.9 convolution_subtract_fusion.8
  59.8 5.7 convolution_add_fusion.8
  68.0 334.9 %reduce-scatter.6.cloned.1.call-done = f32[8,256]{1,0:T(8,128)} async-done(((f32[512,256]{1,0:T(8,128)}), f32[8,256]{1,0:T(8,128)}) %reduce-scatter.6.cloned.1.call-update) | async-done | bytes 8208 | tf_op jit(solution)/shard_map/reduce_scatter | solution.py:86
  403.6 19.6 %all_to_all.10 = f32[64,8,256]{2,1,0:T(8,128)S(1)} all-to-all(f32[64,8,256]{2,1,0:T(8,128)S(1)} %stack.8), channel_id=1, replica_groups=mesh['depth'=64,'comp'=4] {'depth'}, dimensions={0} | all-to-all | bytes 1048576 | tf_op jit(solution)/shard_map/all_to_all | solution.py:104
  443.2 6.0 convolution_subtract_fusion.7
  467.4 5.7 convolution_add_fusion.6
  475.6 71.0 %reduce-scatter.8.cloned.1.call-done = f32[1,128,256]{2,1,0:T(8,128)} async-done(((f32[1,512,256]{2,1,0:T(8,128)}), f32[1,128,256]{2,1,0:T(8,128)}) %reduce-scatter.8.cloned.1.call-update) | async-done | bytes 131088 | tf_op jit(solution)/shard_map/reduce_scatter | solution.py:117
  548.2 7.3 all_gather.10
  575.5 6.0 convolution_subtract_fusion.5
  599.8 5.9 convolution_add_fusion.4
  608.1 333.7 %reduce-scatter.10.cloned.1.call-done = f32[8,256]{1,0:T(8,128)} async-done(((f32[512,256]{1,0:T(8,128)}), f32[8,256]{1,0:T(8,128)}) %reduce-scatter.10.cloned.1.call-update) | async-done | bytes 8208 | tf_op jit(solution)/shard_map/reduce_scatter | solution.py:86
  943.2 124.5 %all-reduce.1 = (f32[]{:T(128)}, f32[]{:T(128)}, f32[]{:T(128)}) all-reduce(f32[]{:T(128)} %get-tuple-element.5, f32[]{:T(128)} %fusion.131, f32[]{:T(128)} %get-tuple-element.4), channel_id=1, replica_groups=mesh['depth'=64,'comp'=4] {'depth','comp'}, use_global_device_ids=true, to_apply=%region_3.4 | all-reduce | flops 3 | bytes 24 | tf_op jit(solution)/shard_map/psum | solution.py:123
  1069.6 23.3 %all_to_all.11 = f32[64,8,256]{2,1,0:T(8,128)S(1)} all-to-all(f32[64,8,256]{2,1,0:T(8,128)S(1)} %stack.10), channel_id=1, replica_groups=mesh['depth'=64,'comp'=4] {'depth'}, dimensions={0} | all-to-all | bytes 1048576 | tf_op jit(solution)/shard_map/all_to_all | solution.py:104
  1112.9 5.8 convolution_subtract_fusion.3
  1129.7 5.7 convolution_subtract_fusion.2
  1137.0 5.9 convolution_add_fusion.2
  1145.3 19.0 %reduce-scatter.12.cloned.1.call-done = f32[1,128,256]{2,1,0:T(8,128)} async-done(((f32[1,512,256]{2,1,0:T(8,128)}), f32[1,128,256]{2,1,0:T(8,128)}) %reduce-scatter.12.cloned.1.call-update) | async-done | bytes 131088 | tf_op jit(solution)/shard_map/reduce_scatter | solution.py:117
  1166.0 7.3 all_gather.11
  1193.2 5.8 convolution_subtract_fusion.1
  1210.0 5.7 convolution_subtract_fusion
  1217.3 5.8 convolution_add_fusion
  1225.4 334.2 %reduce-scatter.14.cloned.1.call-done = f32[8,256]{1,0:T(8,128)} async-done(((f32[512,256]{1,0:T(8,128)}), f32[8,256]{1,0:T(8,128)}) %reduce-scatter.14.cloned.1.call-update) | async-done | bytes 8208 | tf_op jit(solution)/shard_map/reduce_scatter | solution.py:86
  1560.9 124.0 %all-reduce = (f32[]{:T(128)}, f32[]{:T(128)}, f32[]{:T(128)}) all-reduce(f32[]{:T(128)} %get-tuple-element.3, f32[]{:T(128)} %fusion.129, f32[]{:T(128)} %get-tuple-element.2), channel_id=1, replica_groups=mesh['depth'=64,'comp'=4] {'depth','comp'}, use_global_device_ids=true, to_apply=%region_11.12 | all-reduce | flops 3 | bytes 24 | tf_op jit(solution)/shard_map/psum | solution.py:123
  (83 shorter events, 197.4 us)
Async XLA Ops:
  7.2 395.7 %reduce-scatter.6.cloned.1.call-start = ((), (), s32[]{:S(2)}) async-start(), calls=%async_computation.7 | async-start | bytes 532480 | tf_op jit(solution)/shard_map/reduce_scatter | solution.py:86
  67.9 334.9 %copy-start.1 = (f32[1,8,256]{2,1,0:T(8,128)S(1)}, f32[1,8,256]{2,1,0:T(8,128)}, u32[]{:S(2)}) copy-start(f32[1,8,256]{2,1,0:T(8,128)} %param.6) | copy-start | bytes 24580
  67.9 334.9 %copy-start.3 = (f32[1,8,256]{2,1,0:T(8,128)S(1)}, f32[1,8,256]{2,1,0:T(8,128)}, u32[]{:S(2)}) copy-start(f32[1,8,256]{2,1,0:T(8,128)} %param.5) | copy-start | bytes 24580
  67.9 478.7 %reduce-scatter.8.cloned.1.call-start = ((), (), s32[]{:S(2)}) async-start(), calls=%async_computation.8 | async-start | bytes 655360 | tf_op jit(solution)/shard_map/reduce_scatter | solution.py:117
  475.5 71.1 %copy-start = (f32[1,128,256]{2,1,0:T(8,128)S(1)}, f32[1,128,256]{2,1,0:T(8,128)}, u32[]{:S(2)}) copy-start(f32[1,128,256]{2,1,0:T(8,128)} %param.4) | copy-start | bytes 393220
  475.5 466.3 %reduce-scatter.10.cloned.1.call-start = ((), (), s32[]{:S(2)}) async-start(), calls=%async_computation.9 | async-start | bytes 532480 | tf_op jit(solution)/shard_map/reduce_scatter | solution.py:86
  608.1 556.3 %reduce-scatter.12.cloned.1.call-start = ((), (), s32[]{:S(2)}) async-start(), calls=%async_computation.10 | async-start | bytes 655360 | tf_op jit(solution)/shard_map/reduce_scatter | solution.py:117
  943.2 126.3 %copy-start.4 = (f32[8,256]{1,0:T(8,128)S(1)}, f32[8,256]{1,0:T(8,128)}, u32[]{:S(2)}) copy-start(f32[8,256]{1,0:T(8,128)} %reduce-scatter.6.cloned.1.call-done) | copy-start | bytes 24580
  943.2 126.3 %copy-start.2 = (f32[8,256]{1,0:T(8,128)S(1)}, f32[8,256]{1,0:T(8,128)}, u32[]{:S(2)}) copy-start(f32[8,256]{1,0:T(8,128)} %reduce-scatter.10.cloned.1.call-done) | copy-start | bytes 24580
  1145.3 414.3 %reduce-scatter.14.cloned.1.call-start = ((), (), s32[]{:S(2)}) async-start(), calls=%async_computation.11 | async-start | bytes 532480 | tf_op jit(solution)/shard_map/reduce_scatter | solution.py:86
  1686.8 0.7 copy-start.5
Sparse Core Ops, SparseCore 0:
  68.0 334.7 reduce-scatter.5
  475.7 70.9 reduce-scatter.7
  608.2 333.5 reduce-scatter.9
  1145.4 18.9 reduce-scatter.11
  1225.6 334.0 reduce-scatter.13
